TPU v7x, 512 devices: a whole 4x4x16 slice. The times are simulated.
512 devices in a mesh: neuron: 128 (over z, y, core), trial: 4 (over x).
Axes of the slice: x: 4, y: 4, z: 16, core: 2. Of those that a mesh axis runs over, the one named last changes fastest.
Arguments:
- tensor: bfloat16 [8, 16384, 1024], P('trial', 'neuron'), may hold values from -1000 to 1000
- time_init: float32 [32, 1024], replicated, may hold values from -6 to 6
- trial_init: float32 [32, 8], P(None, 'trial'), may hold values from -6 to 6
Outputs:
- neuron_factor: float32 [32, 16384], P(None, 'neuron')
- time_factor: float32 [32, 1024], P(None, ('neuron', 'trial'))
- trial_factor: float32 [32, 8], P(None, 'trial')
All inputs are finite; a program needn't handle non-finite values.
Results may differ from a plain program's by a relative error of at most 0.011.
Values may be sent and summed in bfloat16 or wider, within the bound.
No kernel may reach another device: no remote copies, remote signals or barrier semaphores. Data moves between devices by JAX's collectives and lax.ppermute only.
A program may use at most 64 MiB of HBM per device.

v0:
```python
import jax
import jax.numpy as jnp
from jax import lax
from jax.sharding import PartitionSpec as P

SWEEPS = 2
ridge_share = 0.1
tiny_eps = 1e-06


def gram_of(matrix):
    return lax.dot_general(
        matrix,
        matrix,
        (((1,), (1,)), ((), ())),
        precision=lax.Precision.HIGHEST,
        preferred_element_type=jnp.float32,
    )


def damped_solve(gram_mat, right_hand):
    order_size = gram_mat.shape[0]
    identity_mat = jnp.eye(order_size, dtype=jnp.float32)
    damped = gram_mat + ridge_share * (jnp.trace(gram_mat) / order_size) * identity_mat
    cholesky_low = jnp.linalg.cholesky(damped)
    return jax.scipy.linalg.cho_solve((cholesky_low, True), right_hand)


def per_device(tensor, time_init, trial_init):
    timepoints = tensor.shape[2]
    component_count = time_init.shape[0]
    neuron_count = tensor.shape[1] * lax.axis_size("neuron")
    devices = lax.axis_size("neuron") * lax.axis_size("trial")
    share_width = timepoints // devices
    position = lax.axis_index(("neuron", "trial"))

    def trial_gram_of(trial_cols):
        return gram_of(lax.all_gather(trial_cols, "trial", axis=1, tiled=True))

    trial_now = trial_init
    trial_gram = trial_gram_of(trial_now)
    time_gram = gram_of(time_init)
    time_rounded = time_init.astype(jnp.bfloat16)
    time_out = lax.dynamic_slice_in_dim(time_init, position * share_width, share_width, 1)
    neuron_now = jnp.zeros((component_count, tensor.shape[1]), jnp.float32)
    for sweep_index in range(SWEEPS):
        projected = jnp.einsum(
            "rj,kij->kri", time_rounded, tensor, preferred_element_type=jnp.float32
        )
        local_terms = jnp.sum(trial_now.T[:, :, None] * projected, axis=0)
        neuron_terms = lax.psum(local_terms, "trial")
        neuron_raw = damped_solve(trial_gram * time_gram, neuron_terms)
        squares = lax.psum(jnp.sum(neuron_raw * neuron_raw, axis=1), "neuron")
        scaling = 1.0 / jnp.sqrt(squares / neuron_count + tiny_eps)
        neuron_now = neuron_raw * scaling[:, None]
        neuron_gram, trial_terms = lax.psum(
            (gram_of(neuron_now), jnp.sum(neuron_now[None] * projected, axis=2).T), "neuron"
        )
        trial_now = damped_solve(neuron_gram * time_gram, trial_terms)
        trial_gram = trial_gram_of(trial_now)
        weights = (neuron_now[None] * trial_now.T[:, :, None]).astype(jnp.bfloat16)
        time_local = jnp.einsum("kri,kij->rj", weights, tensor, preferred_element_type=jnp.float32)
        time_system = neuron_gram * trial_gram
        time_terms = lax.psum(time_local, ("neuron", "trial"))
        time_raw = damped_solve(time_system, time_terms)
        time_now = time_raw / jnp.sqrt(
            jnp.mean(time_raw * time_raw, axis=1, keepdims=True) + tiny_eps
        )
        time_gram = gram_of(time_now)
        time_rounded = time_now.astype(jnp.bfloat16)
        time_out = lax.dynamic_slice_in_dim(time_now, position * share_width, share_width, 1)
    return (neuron_now, time_out, trial_now)


def solution(mesh):
    placed = (P("trial", "neuron", None), P(), P(None, "trial"))
    return jax.shard_map(
        per_device,
        mesh=mesh,
        in_specs=placed,
        out_specs=(P(None, "neuron"), P(None, ("neuron", "trial")), P(None, "trial")),
        check_vma=False,
    )
```

profile of v0, /device:TPU:1, one launch (start us, length us, event | category | flops | bytes accessed | tf_op | source)
XLA Modules:
  0.0 2487.0 jit_solution(9856906988820335533)
XLA Ops:
  7.2 1.3 fusion.51
  8.5 8.7 all-gather
  17.2 0.8 select_reduce_fusion.8
  18.8 2.9 cholesky.104
  21.7 0.6 compare_reduce_fusion.5
  22.4 0.7 fusion.5
  23.0 2.4 custom-call.20
  25.8 11.0 psum.70
  37.3 259.1 %psum.71 = f32[32]{0:T(128)S(1)} all-reduce(f32[32]{0:T(128)S(1)} %get-tuple-element.29), channel_id=1, replica_groups=mesh['neuron'=128,'trial'=4] {'neuron'}, use_global_device_ids=true, to_apply=%region_6.9 | all-reduce | flops 32 | bytes 256 | tf_op jit(solution)/shard_map/psum | solution.py:53
  296.7 485.7 %all-reduce.1 = (f32[32,2]{0,1:T(2,128)S(1)}, f32[32,32]{0,1:T(8,128)S(1)}) all-reduce(f32[32,2]{0,1:T(2,128)S(1)} %bitcast.141, f32[32,32]{0,1:T(8,128)S(1)} %fusion.52), channel_id=1, replica_groups=mesh['neuron'=128,'trial'=4] {'neuron'}, use_global_device_ids=true, to_apply=%region_10.13 | all-reduce | flops 1088 | bytes 8704 | tf_op jit(solution)/shard_map/psum | solution.py:56
  782.4 0.6 select_reduce_fusion.7
  783.8 2.9 cholesky.115
  786.7 0.6 compare_reduce_fusion.4
  787.3 0.7 fusion.6
  788.0 2.4 custom-call.21
  790.9 0.9 convolution_bitcast_fusion.1
  791.9 6.2 all-gather.1
  798.1 0.8 select_reduce_fusion.6
  799.7 2.9 cholesky.126
  802.6 0.6 compare_reduce_fusion.3
  803.3 0.7 fusion.7
  803.9 2.4 custom-call.22
  806.4 440.6 %all-reduce.5.cloned.1.call-done = f32[32,1024]{1,0:T(8,128)} async-done(((f32[32,1024]{1,0:T(8,128)}), f32[32,1024]{1,0:T(8,128)}) %all-reduce.5.cloned.1.call-update) | async-done | bytes 131088 | tf_op jit(solution)/shard_map/psum | solution.py:64
  1246.9 1.2 fusion.28
  1248.8 1.0 select_reduce_fusion.5
  1250.5 2.9 cholesky.137
  1253.5 0.6 compare_reduce_fusion.2
  1254.1 0.7 fusion.8
  1254.8 2.4 custom-call.23
  1257.2 12.2 psum.75
  1269.8 249.2 %psum.76 = f32[32]{0:T(128)S(1)} all-reduce(f32[32]{0:T(128)S(1)} %get-tuple-element.37), channel_id=1, replica_groups=mesh['neuron'=128,'trial'=4] {'neuron'}, use_global_device_ids=true, to_apply=%region_18.23 | all-reduce | flops 32 | bytes 256 | tf_op jit(solution)/shard_map/psum | solution.py:53
  1519.3 485.9 %all-reduce = (f32[32,2]{0,1:T(2,128)S(1)}, f32[32,32]{0,1:T(8,128)S(1)}) all-reduce(f32[32,2]{0,1:T(2,128)S(1)} %bitcast.142, f32[32,32]{0,1:T(8,128)S(1)} %fusion.53), channel_id=1, replica_groups=mesh['neuron'=128,'trial'=4] {'neuron'}, use_global_device_ids=true, to_apply=%region_22.27 | all-reduce | flops 1088 | bytes 8704 | tf_op jit(solution)/shard_map/psum | solution.py:56
  2005.2 0.6 select_reduce_fusion.4
  2006.6 2.9 cholesky.148
  2009.5 0.6 compare_reduce_fusion.1
  2010.2 0.7 fusion.9
  2010.8 2.4 custom-call.24
  2013.7 5.3 all-gather.2
  2019.0 0.8 select_reduce_fusion.3
  2020.5 2.9 cholesky.159
  2023.5 0.6 compare_reduce_fusion
  2024.1 0.9 convolution_bitcast_fusion
  2025.0 0.7 fusion.10
  2025.7 2.4 custom-call.25
  2028.1 449.7 %all-reduce.7.cloned.1.call-done = f32[32,1024]{1,0:T(8,128)} async-done(((f32[32,1024]{1,0:T(8,128)}), f32[32,1024]{1,0:T(8,128)}) %all-reduce.7.cloned.1.call-update) | async-done | bytes 131088 | tf_op jit(solution)/shard_map/psum | solution.py:64
  2477.9 1.2 fusion.13
  2479.1 0.4 multiply_reduce_fusion
  2479.6 0.6 copy.39
  (60 shorter events, 4.3 us)
Async XLA Ops:
  7.2 18.3 copy-start
  7.2 1239.8 %all-reduce.5.cloned.1.call-start = ((), (), s32[]{:S(2)}) async-start(), calls=%async_computation | async-start | bytes 262144 | tf_op jit(solution)/shard_map/psum | solution.py:64
  7.2 1.3 copy-start.4
  8.5 16.9 copy-start.1
  791.8 1686.1 %all-reduce.7.cloned.1.call-start = ((), (), s32[]{:S(2)}) async-start(), calls=%async_computation.1 | async-start | bytes 262144 | tf_op jit(solution)/shard_map/psum | solution.py:64
  1519.1 505.0 %copy-start.2 = (f32[32,128]{1,0:T(8,128)}, f32[32,128]{1,0:T(8,128)S(1)}, u32[]{:S(2)}) copy-start(f32[32,128]{1,0:T(8,128)S(1)} %broadcast_multiply_fusion) | copy-start | bytes 49156
  2013.7 10.4 copy-start.3
Sparse Core Ops, SparseCore 0:
  791.9 454.9 all-reduce.4
  2025.2 452.6 all-reduce.6
where the time goes:
time: 2490 us
  blocking collectives  1520 us (61%)
  waiting for transfers between devices  890 us (36%)
  other arithmetic  41.8 us (2%)
    psum x2, blocking collectives, per_device(): lax.psum((gram_of(neuron_now), jnp.sum(neuron_now[None] * projected, axis...  972 us
    psum x2, waiting for transfers between devices, per_device(): time_terms = lax.psum(time_local, ('neuron', 'trial'))  890 us
    psum x2, blocking collectives, per_device(): squares = lax.psum(jnp.sum(neuron_raw * neuron_raw, axis=1), 'neuron')  508 us
  transfers between devices with their start and end apart: 2, of which 2 were waited for; matrix products, arithmetic and copies ran while one was open for 0% of the time, Pallas kernels for 0%

commit v1 on v0

--- a/solution.py
+++ b/solution.py
@@ -61,7 +61,7 @@
         weights = (neuron_now[None] * trial_now.T[:, :, None]).astype(jnp.bfloat16)
         time_local = jnp.einsum("kri,kij->rj", weights, tensor, preferred_element_type=jnp.float32)
         time_system = neuron_gram * trial_gram
-        time_terms = lax.psum(time_local, ("neuron", "trial"))
+        time_terms = jax.lax.psum(jax.lax.psum(time_local, "trial"), "neuron")
         time_raw = damped_solve(time_system, time_terms)
         time_now = time_raw / jnp.sqrt(
             jnp.mean(time_raw * time_raw, axis=1, keepdims=True) + tiny_eps

time: 2490 us -> 2350 us (0.944)
  waiting for transfers between devices: 890 us -> 746 us
    psum x2 -> x4, waiting for transfers between devices: 890 us -> 746 us  [per_device(): time_terms = jax.lax.psum(jax.lax.psum(time_local, 'trial'), 'neuron')]
  transfers between devices with their start and end apart: 2 -> 4, of which waited for: 2 -> 4; matrix products, arithmetic and copies ran while one was open for 0% -> 0% of each run, Pallas kernels for 0% -> 0%
where the time goes in v1:
time: 2350 us
  blocking collectives  1530 us (65%)
  waiting for transfers between devices  746 us (32%)
  other arithmetic  41.8 us (2%)
    psum x2, blocking collectives, per_device(): lax.psum((gram_of(neuron_now), jnp.sum(neuron_now[None] * projected, axis...  972 us
    psum x4, waiting for transfers between devices, per_device(): time_terms = jax.lax.psum(jax.lax.psum(time_local, 'trial'), 'neuron')  746 us
    psum x2, blocking collectives, per_device(): squares = lax.psum(jnp.sum(neuron_raw * neuron_raw, axis=1), 'neuron')  511 us
  transfers between devices with their start and end apart: 4, of which 4 were waited for; matrix products, arithmetic and copies ran while one was open for 0% of the time, Pallas kernels for 0%

profile of v1, /device:TPU:1, one launch (start us, length us, event | category | flops | bytes accessed | tf_op | source)
XLA Modules:
  0.0 2346.4 jit_solution(16221688963698033494)
XLA Ops:
  7.2 1.3 fusion.51
  8.5 8.7 all-gather
  17.2 0.8 select_reduce_fusion.8
  18.8 2.9 cholesky.104
  21.7 0.6 compare_reduce_fusion.5
  22.4 0.7 fusion.5
  23.0 2.4 custom-call.20
  25.8 11.0 psum.84
  37.3 259.1 %psum.85 = f32[32]{0:T(128)S(1)} all-reduce(f32[32]{0:T(128)S(1)} %get-tuple-element.29), channel_id=1, replica_groups=mesh['neuron'=128,'trial'=4] {'neuron'}, use_global_device_ids=true, to_apply=%region_6.9 | all-reduce | flops 32 | bytes 256 | tf_op jit(solution)/shard_map/psum | solution.py:53
  296.7 485.7 %all-reduce.1 = (f32[32,2]{0,1:T(2,128)S(1)}, f32[32,32]{0,1:T(8,128)S(1)}) all-reduce(f32[32,2]{0,1:T(2,128)S(1)} %bitcast.141, f32[32,32]{0,1:T(8,128)S(1)} %fusion.52), channel_id=1, replica_groups=mesh['neuron'=128,'trial'=4] {'neuron'}, use_global_device_ids=true, to_apply=%region_10.13 | all-reduce | flops 1088 | bytes 8704 | tf_op jit(solution)/shard_map/psum | solution.py:56
  783.8 2.9 cholesky.115
  786.7 0.6 compare_reduce_fusion.4
  787.3 0.7 fusion.6
  788.0 2.4 custom-call.21
  790.9 0.9 convolution_bitcast_fusion.1
  791.9 6.2 all-gather.1
  798.1 0.8 select_reduce_fusion.6
  799.7 2.9 cholesky.126
  802.6 0.6 compare_reduce_fusion.3
  803.3 41.8 %all-reduce.7.cloned.1.call-done = f32[32,1024]{1,0:T(8,128)} async-done(((f32[32,1024]{1,0:T(8,128)}), f32[32,1024]{1,0:T(8,128)}) %all-reduce.7.cloned.1.call-update) | async-done | bytes 131088 | tf_op jit(solution)/shard_map/psum | solution.py:64
  845.1 0.7 fusion.7
  845.8 2.4 custom-call.22
  848.2 326.9 %all-reduce.9.cloned.1.call-done = f32[32,1024]{1,0:T(8,128)} async-done(((f32[32,1024]{1,0:T(8,128)}), f32[32,1024]{1,0:T(8,128)}) %all-reduce.9.cloned.1.call-update) | async-done | bytes 131088 | tf_op jit(solution)/shard_map/psum | solution.py:64
  1175.1 1.2 fusion.28
  1176.9 1.0 select_reduce_fusion.5
  1178.6 2.9 cholesky.137
  1181.6 0.6 compare_reduce_fusion.2
  1182.2 0.7 fusion.8
  1182.9 2.4 custom-call.23
  1185.3 13.3 psum.90
  1199.1 252.3 %psum.91 = f32[32]{0:T(128)S(1)} all-reduce(f32[32]{0:T(128)S(1)} %get-tuple-element.37), channel_id=1, replica_groups=mesh['neuron'=128,'trial'=4] {'neuron'}, use_global_device_ids=true, to_apply=%region_19.24 | all-reduce | flops 32 | bytes 256 | tf_op jit(solution)/shard_map/psum | solution.py:53
  1451.7 485.9 %all-reduce = (f32[32,2]{0,1:T(2,128)S(1)}, f32[32,32]{0,1:T(8,128)S(1)}) all-reduce(f32[32,2]{0,1:T(2,128)S(1)} %bitcast.142, f32[32,32]{0,1:T(8,128)S(1)} %fusion.53), channel_id=1, replica_groups=mesh['neuron'=128,'trial'=4] {'neuron'}, use_global_device_ids=true, to_apply=%region_23.28 | all-reduce | flops 1088 | bytes 8704 | tf_op jit(solution)/shard_map/psum | solution.py:56
  1937.6 0.6 select_reduce_fusion.4
  1939.0 2.9 cholesky.148
  1941.9 0.6 compare_reduce_fusion.1
  1942.6 0.7 fusion.9
  1943.2 2.4 custom-call.24
  1946.1 5.3 all-gather.2
  1951.4 0.8 select_reduce_fusion.3
  1952.9 2.9 cholesky.159
  1955.9 0.9 convolution_bitcast_fusion
  1956.9 0.6 compare_reduce_fusion
  1957.5 50.2 %all-reduce.11.cloned.1.call-done = f32[32,1024]{1,0:T(8,128)} async-done(((f32[32,1024]{1,0:T(8,128)}), f32[32,1024]{1,0:T(8,128)}) %all-reduce.11.cloned.1.call-update) | async-done | bytes 131088 | tf_op jit(solution)/shard_map/psum | solution.py:64
  2007.8 0.7 fusion.10
  2008.4 2.4 custom-call.25
  2010.9 326.7 %all-reduce.13.cloned.1.call-done = f32[32,1024]{1,0:T(8,128)} async-done(((f32[32,1024]{1,0:T(8,128)}), f32[32,1024]{1,0:T(8,128)}) %all-reduce.13.cloned.1.call-update) | async-done | bytes 131088 | tf_op jit(solution)/shard_map/psum | solution.py:64
  2337.5 1.2 fusion.13
  2339.2 0.6 copy.39
  (66 shorter events, 5.4 us)
Async XLA Ops:
  7.2 18.3 copy-start
  7.2 837.9 %all-reduce.7.cloned.1.call-start = ((), (), s32[]{:S(2)}) async-start(), calls=%async_computation | async-start | bytes 262144 | tf_op jit(solution)/shard_map/psum | solution.py:64
  7.2 1.3 copy-start.4
  8.5 16.9 copy-start.1
  791.8 383.3 %all-reduce.9.cloned.1.call-start = ((), (), s32[]{:S(2)}) async-start(), calls=%async_computation.1 | async-start | bytes 262144 | tf_op jit(solution)/shard_map/psum | solution.py:64
  845.1 1162.7 %all-reduce.11.cloned.1.call-start = ((), (), s32[]{:S(2)}) async-start(), calls=%async_computation.2 | async-start | bytes 262144 | tf_op jit(solution)/shard_map/psum | solution.py:64
  1451.5 504.4 %copy-start.2 = (f32[32,128]{1,0:T(8,128)}, f32[32,128]{1,0:T(8,128)S(1)}, u32[]{:S(2)}) copy-start(f32[32,128]{1,0:T(8,128)S(1)} %broadcast_multiply_fusion) | copy-start | bytes 49156
  1946.1 9.8 copy-start.3
  1956.8 380.8 %all-reduce.13.cloned.1.call-start = ((), (), s32[]{:S(2)}) async-start(), calls=%async_computation.3 | async-start | bytes 262144 | tf_op jit(solution)/shard_map/psum | solution.py:64
Sparse Core Ops, SparseCore 0:
  791.9 53.0 all-reduce.6
  848.5 326.5 all-reduce.8
  1956.9 50.7 all-reduce.10
  2011.0 326.4 all-reduce.12
